TPU v7x, 32 devices: a whole 2x2x4 slice. The times are simulated.
32 devices in a mesh: slab: 8 (over z, x), freq: 4 (over y, core).
Axes of the slice: x: 2, y: 2, z: 4, core: 2. Of those that a mesh axis runs over, the one named last changes fastest.
Arguments:
- partials: bfloat16 [8, 3, 2, 32, 32, 5, 256], P('slab', None, None, 'freq'), may hold values from -400 to 400
- rec_plane: int32 [8, 3, 2], P('slab'), may hold values from 0 to 1
- rec_count: int32 [8, 3], P('slab'), may hold values from 0 to 2, as said below
- rec_weight: bfloat16 [8, 3, 2, 256], P('slab'), may hold values from 0.25 to 1
- qweight: float32 [16, 256], P('slab'), as said below
Outputs:
- spectra: bfloat16 [8, 32, 2, 16, 5, 256], P('freq', None, None, 'slab')
- r_factor: float32 [8, 64, 64], P('freq')
Inputs may be any that keep to these rules, and one draw needn't show every extreme that they name: `rec_count`: at most 2 live records from one source to one destination, reached in every draw; a source's records to its own index number exactly 2; none leave the ends of the slab axis; some destination receives 2 from each of its three sources. `qweight`: positive.
All inputs are finite; a program needn't handle non-finite values.
Results may differ from a plain program's by a relative error of at most 0.0025.
The roundings to bfloat16 on the way count: a program that leaves them out, or rounds other values in their place, can miss the bound.
Values may be sent and summed in bfloat16 or wider, within the bound.
No kernel may reach another device: no remote copies, remote signals or barrier semaphores. Data moves between devices by JAX's collectives and lax.ppermute only.
A program may use at most 64 MiB of HBM per device.

v0:
```python
import math
import jax
import jax.numpy as jnp
from jax import lax
from jax.sharding import PartitionSpec as P

NT = 32
NY = 16
NZ = 16
NF = 8
TAPS = (-0.0625, 0.25, 0.625, 0.25, -0.0625)


def from_behind(value, axis, steps):
    count = lax.axis_size(axis)
    leading, last = (max(0, -steps), min(count, count - steps))
    return lax.ppermute(value, axis, [(source, source + steps) for source in range(leading, last)])


def padded_2(block, sides, width):
    for axis, dim in sides:
        count = lax.axis_size(axis)
        forward = [(i, i + 1) for i in range(count - 1)]
        backward = [(target, source) for source, target in forward]
        low = lax.ppermute(
            lax.slice_in_dim(block, block.shape[dim] - width, None, axis=dim), axis, forward
        )
        high = lax.ppermute(lax.slice_in_dim(block, 0, width, axis=dim), axis, backward)
        block = jnp.concatenate([low, block, high], axis=dim)
    return block


def band_matrix(size):
    index = jnp.arange(size)
    offset = index[None, :] - index[:, None]
    result = jnp.zeros((size, size), jnp.float32)
    for place in range(5):
        result = result + TAPS[place] * (offset == place - 2).astype(jnp.float32)
    return result


def dft_table():
    times = jnp.arange(NT).astype(jnp.float32)
    freqs = jnp.arange(NF).astype(jnp.float32) + 1.0
    window = 0.5 - 0.5 * jnp.cos(2.0 * math.pi * times / NT)
    factor = 1.0 / jnp.sqrt(jnp.sum(window * window))
    angle = 2.0 * math.pi * times[:, None] * freqs[None, :] / NT
    real_part = factor * window[:, None] * jnp.cos(angle)
    imag_part = -factor * window[:, None] * jnp.sin(angle)
    return jnp.stack([real_part, imag_part], axis=2)


def record_terms(pieces, weights, planes, counts, plane_total):
    slots = jnp.arange(pieces.shape[0])
    valid = slots < counts[0]
    select = ((planes[:, None] == jnp.arange(plane_total)[None, :]) & valid[:, None]).astype(
        jnp.float32
    )
    scaled = pieces.astype(jnp.float32) * weights.astype(jnp.float32)[:, None, None, None, :]
    return jnp.einsum("cq,cbtvp->qbtvp", select, scaled, precision=lax.Precision.HIGHEST)


def upper_factor(gram):
    return jnp.swapaxes(jnp.linalg.cholesky(gram), 1, 2)


def add_products(total, piece):
    return total + jnp.einsum("akij,akil->kjl", piece, piece, precision=lax.Precision.HIGHEST)


def body(partials, rec_plane, rec_count, rec_weight, qweight):
    plane_total = qweight.shape[0]
    points = qweight.shape[1]

    def side_terms(side):
        return record_terms(
            partials[0, side],
            rec_weight[0, side],
            rec_plane[0, side],
            rec_count[0, side : side + 1],
            plane_total,
        )

    total = side_terms(1)
    total = total + from_behind(side_terms(0), "slab", -1)
    total = total + from_behind(side_terms(2), "slab", 1)
    assembled = total.astype(jnp.bfloat16)
    padded = padded_2(assembled, (("slab", 0),), 2)
    kyz = jnp.kron(band_matrix(NY), band_matrix(NZ)).astype(jnp.bfloat16)
    across = jnp.dot(padded.reshape(-1, points), kyz, preferred_element_type=jnp.float32).reshape(
        padded.shape
    )
    smoothed = TAPS[0] * across[0:plane_total]
    for place in range(1, 5):
        smoothed = smoothed + TAPS[place] * across[place : place + plane_total]
    local_spec = jnp.einsum(
        "xbtvp,tkr->kbrxvp", smoothed, dft_table(), precision=lax.Precision.HIGHEST
    ).astype(jnp.bfloat16)
    spectra = lax.all_to_all(local_spec, "freq", split_axis=0, concat_axis=1, tiled=True)
    freq_count = spectra.shape[0]
    columns = 2 * spectra.shape[1]
    values = spectra.astype(jnp.float32).reshape(
        freq_count, columns, plane_total, spectra.shape[4], points
    )
    weighted = (values * qweight[None, None, :, None, :]).reshape(freq_count, columns, -1)
    flat_values = values.reshape(freq_count, columns, -1)
    gram = jnp.einsum("kcr,kdr->kcd", weighted, flat_values, precision=lax.Precision.HIGHEST)
    local_factor = upper_factor(gram)[None]
    empty = jnp.zeros(gram.shape, jnp.float32)
    summed = add_products(
        empty,
        lax.all_gather(local_factor.astype(jnp.bfloat16), "slab", axis=0, tiled=True).astype(
            jnp.float32
        ),
    )
    factor = upper_factor(summed)
    return (spectra, factor)


def solution(mesh):
    placed = (
        P("slab", None, None, "freq", None, None, None),
        P("slab", None, None),
        P("slab", None),
        P("slab", None, None, None),
        P("slab", None),
    )
    return jax.shard_map(
        body,
        mesh=mesh,
        in_specs=placed,
        out_specs=(P("freq", None, None, "slab", None, None), P("freq", None, None)),
        check_vma=False,
    )
```

profile of v0, /device:TPU:0, one launch (start us, length us, event | category | flops | bytes accessed | tf_op | source)
XLA Modules:
  0.0 303.7 jit_solution(14255040084964306091)
XLA Ops:
  0.6 0.7 bitcast_convert_fusion.2
  1.3 1.4 fusion.54
  2.8 0.7 iota_compare_fusion.3
  3.5 1.0 slice_reduce_fusion.2
  4.5 3.2 %convert_multiply_fusion.2 = (f32[2,8,32,5,256]{4,2,3,1,0:T(8,128)S(1)}, f32[2,8,32,5,256]{4,2,3,1,0:T(8,128)S(1)}, f32[2,8,32,5,256]{4,2,3,1,0:T(8,128)S(1)}) fusion(f32[2,256]{1,0:T(2,128)S(1)} %get-tuple-element.19, bf16[1,3,2,8,32,5,256]{6,4,5,3,2,1,0:T(8,128)(2,1)} %param.6, f32[2,256]{1,0:T(2,128)S(1)} %get-tuple-element.20, ...), kind=kLoop, calls=%fused_computation.12 | loop fusion | flops 3932160 | bytes 11802624 | tf_op jit(solution)/shard_map/mul | solution.py:59
  7.7 5.8 %fusion.9 = f32[2,8,32,5,256]{4,0,3,2,1:T(2,128)S(1)} fusion(f32[2,8,32,5,256]{4,2,3,1,0:T(8,128)S(1)} %get-tuple-element.18, pred[2]{0:T(512)(128)(4,1)S(1)} %iota_compare_fusion.3, s32[2]{0:T(128)S(1)} %get-tuple-element.15), kind=kOutput, calls=%fused_computation.19 | convolution fusion | flops 15728648 | bytes 5242890 | tf_op jit(solution)/shard_map/cq,cbtvp->qbtvp/dot_general | solution.py:60
  13.6 1.3 collective-permute-start
  14.9 0.7 iota_compare_fusion.2
  15.5 5.8 %fusion.7 = f32[2,8,32,5,256]{4,0,3,2,1:T(2,128)S(1)} fusion(f32[2,8,32,5,256]{4,2,3,1,0:T(8,128)S(1)} %get-tuple-element.17, pred[2]{0:T(512)(128)(4,1)S(1)} %iota_compare_fusion.2, s32[2]{0:T(128)S(1)} %get-tuple-element.14), kind=kOutput, calls=%fused_computation.17 | convolution fusion | flops 15728648 | bytes 5242890 | tf_op jit(solution)/shard_map/cq,cbtvp->qbtvp/dot_general | solution.py:60
  21.4 5.7 %collective-permute-start.1 = (f32[2,8,32,5,256]{4,0,3,2,1:T(2,128)S(1)}, f32[2,8,32,5,256]{4,0,3,2,1:T(2,128)S(1)}, u32[]{:S(2)}, u32[]{:S(2)}) collective-permute-start(f32[2,8,32,5,256]{4,0,3,2,1:T(2,128)S(1)} %fusion.7), channel_id=1, source_target_pairs={{0,4},{4,8},{8,12},{12,16},{16,20},{20,24},{24,28},{1,5},{5,9},{9,... | collective-permute-start | bytes 7864328 | tf_op jit(solution)/shard_map/ppermute | solution.py:17
  27.0 0.7 iota_compare_fusion.4
  27.7 47.6 %collective-permute-done = f32[2,8,32,5,256]{4,0,3,2,1:T(2,128)S(1)} collective-permute-done((f32[2,8,32,5,256]{4,0,3,2,1:T(2,128)S(1)}, f32[2,8,32,5,256]{4,0,3,2,1:T(2,128)S(1)}, u32[]{:S(2)}, u32[]{:S(2)}) %collective-permute-start) | collective-permute-done | bytes 2621472 | tf_op jit(solution)/shard_map/ppermute | solution.py:17
  75.3 56.3 %collective-permute-done.1 = f32[2,8,32,5,256]{4,0,3,2,1:T(2,128)S(1)} collective-permute-done((f32[2,8,32,5,256]{4,0,3,2,1:T(2,128)S(1)}, f32[2,8,32,5,256]{4,0,3,2,1:T(2,128)S(1)}, u32[]{:S(2)}, u32[]{:S(2)}) %collective-permute-start.1) | collective-permute-done | bytes 2621472 | tf_op jit(solution)/shard_map/ppermute | solution.py:17
  131.6 7.8 %add_convert_fusion = bf16[2,8,32,5,256]{4,0,3,2,1:T(2,128)(2,1)S(1)} fusion(f32[2,8,32,5,256]{4,0,3,2,1:T(2,128)S(1)} %collective-permute-done.1, f32[2,8,32,5,256]{4,0,3,2,1:T(2,128)S(1)} %collective-permute-done, f32[2,8,32,5,256]{4,2,3,1,0:T(8,128)S(1)} %get-tuple-element.16, pred[2]{0:T(512)(128)(4,1)S(1)} %iota_compare_fusion.4, ...), kind=kOutput, calls=%fused_computation.16 | convolution fusion | flops 17694728 | bytes 9175050 | tf_op jit(solution)/shard_map/cq,cbtvp->qbtvp/dot_general | solution.py:60
  139.4 5.5 %collective-permute-start.2 = (bf16[2,8,32,5,256]{4,0,3,2,1:T(2,128)(2,1)S(1)}, bf16[2,8,32,5,256]{4,0,3,2,1:T(2,128)(2,1)}, u32[]{:S(2)}, u32[]{:S(2)}) collective-permute-start(bf16[2,8,32,5,256]{4,0,3,2,1:T(2,128)(2,1)S(1)} %add_convert_fusion), channel_id=1, source_target_pairs={{0,4},{4,8},{8,12},{12,16},{16,20},{20,24},{24,28},{1,5},{5,9},{9,... | collective-permute-start | bytes 3932168 | tf_op jit(solution)/shard_map/ppermute | solution.py:25
  144.9 1.5 collective-permute-start.3
  146.4 0.2 multiply_convert_fusion
  146.6 1.0 convert_element_type.143
  147.6 0.7 multiply_reduce_fusion
  149.1 0.1 cosine_multiply_fusion
  149.2 50.9 %collective-permute-done.2 = bf16[2,8,32,5,256]{4,0,3,2,1:T(2,128)(2,1)} collective-permute-done((bf16[2,8,32,5,256]{4,0,3,2,1:T(2,128)(2,1)S(1)}, bf16[2,8,32,5,256]{4,0,3,2,1:T(2,128)(2,1)}, u32[]{:S(2)}, u32[]{:S(2)}) %collective-permute-start.2) | collective-permute-done | bytes 1310752 | tf_op jit(solution)/shard_map/ppermute | solution.py:25
  200.1 0.0 collective-permute-done.3
  200.1 5.7 %pad_maximum_fusion = bf16[6,8,32,5,256]{4,0,3,2,1:T(8,128)(2,1)S(1)} fusion(bf16[2,8,32,5,256]{4,0,3,2,1:T(2,128)(2,1)} %collective-permute-done.3, bf16[2,8,32,5,256]{4,0,3,2,1:T(2,128)(2,1)S(1)} %add_convert_fusion, bf16[2,8,32,5,256]{4,0,3,2,1:T(2,128)(2,1)} %collective-permute-done.2), kind=kLoop, calls=%fused_computation | loop fusion | flops 11796480 | bytes 7864320 | tf_op jit(solution)/shard_map/concatenate | solution.py:29
  205.8 4.1 %copy.59 = bf16[6,8,32,5,256]{4,3,2,1,0:T(8,128)(2,1)} copy(bf16[6,8,32,5,256]{4,0,3,2,1:T(8,128)(2,1)S(1)} %pad_maximum_fusion) | data formatting | bytes 7864320 | tf_op jit(solution)/shard_map/concatenate | solution.py:29
  210.0 8.4 %reshape.309 = bf16[7680,256]{1,0:T(8,128)(2,1)} reshape(bf16[6,8,32,5,256]{4,3,2,1,0:T(8,128)(2,1)} %copy.59) | data formatting | bytes 7864320 | tf_op jit(solution)/shard_map/reshape | solution.py:90
  218.4 3.3 %fusion.55 = f32[7680,256]{1,0:T(8,128)S(1)} fusion(bf16[7680,256]{1,0:T(8,128)(2,1)} %reshape.309, bf16[256,256]{1,0:T(8,128)(2,1)S(1)} %convert_element_type.143), kind=kOutput, calls=%fused_computation.93 | convolution fusion | flops 1006632960 | bytes 11927552 | tf_op jit(solution)/shard_map/dot_general | solution.py:90
  221.7 0.8 fusion
  222.5 2.1 reshape.316
  224.7 0.0 copy-start
  224.7 4.2 %fusion.21 = bf16[8,8,2,2,5,256]{5,0,4,1,3,2:T(8,128)(2,1)S(1)} fusion(f32[2,8,32,5,256]{4,3,2,1,0:T(8,128)} %reshape.316, f32[32,8,1]{0,1,2:T(8,128)S(1)} %get-tuple-element.23, f32[32,8,1]{0,1,2:T(8,128)S(1)} %get-tuple-element.22), kind=kOutput, calls=%fused_computation.28 | convolution fusion | flops 126157312 | bytes 3278848 | tf_op jit(solution)/shard_map/xbtvp,tkr->kbrxvp/dot_general | solution.py:96
  228.9 1.0 copy.61
  229.9 3.7 %all-to-all-start = ((bf16[8,8,2,2,5,256]{5,1,4,3,2,0:T(8,128)(2,1)}), bf16[8,8,2,2,5,256]{5,1,4,3,2,0:T(8,128)(2,1)S(1)}, u32[]{:S(2)}, u32[]{:S(2)}) async-start(bf16[8,8,2,2,5,256]{5,1,4,3,2,0:T(8,128)(2,1)} %copy.61), calls=%async_computation | async-start | bytes 1310720 | tf_op jit(solution)/shard_map/all_to_all | solution.py:99
  233.6 0.0 copy-done
  233.7 9.9 %all-to-all-done = bf16[8,8,2,2,5,256]{5,1,4,3,2,0:T(8,128)(2,1)S(1)} async-done(((bf16[8,8,2,2,5,256]{5,1,4,3,2,0:T(8,128)(2,1)}), bf16[8,8,2,2,5,256]{5,1,4,3,2,0:T(8,128)(2,1)S(1)}, u32[]{:S(2)}, u32[]{:S(2)}) %all-to-all-start) | async-done | bytes 655392 | tf_op jit(solution)/shard_map/all_to_all | solution.py:99
  243.6 0.2 copy.92
  243.8 0.7 all_to_all.19
  244.5 0.8 fusion.18
  245.3 0.1 copy.64
  245.4 11.7 %custom-call.4 = f32[2,64,64]{2,1,0:T(8,128)S(1)} custom-call(f32[2,64,64]{2,1,0:T(8,128)S(1)} %fusion.26), custom_call_target="Cholesky" | custom-call | tf_op jit(solution)/shard_map/jit(cholesky)/cholesky | solution.py:64
  257.2 0.1 compare_reduce_fusion.1
  257.3 0.1 fusion.27
  257.4 0.1 copy.65
  257.5 31.8 %all-gather = bf16[16,64,64]{2,1,0:T(8,128)(2,1)S(1)} all-gather(bf16[2,64,64]{2,1,0:T(8,128)(2,1)S(1)} %copy.65), channel_id=2, replica_groups=mesh['slab'=8,'freq'=4] {'slab'}, dimensions={0}, use_global_device_ids=true | all-gather | bytes 147456 | tf_op jit(solution)/shard_map/all_gather | solution.py:112
  289.3 0.2 convolution_bitcast_fusion
  289.6 0.1 copy.67
  289.7 11.7 %custom-call.5 = f32[2,64,64]{2,1,0:T(8,128)S(1)} custom-call(f32[2,64,64]{2,1,0:T(8,128)S(1)} %fusion.25), custom_call_target="Cholesky" | custom-call | tf_op jit(solution)/shard_map/jit(cholesky)/cholesky | solution.py:64
  301.5 0.1 compare_reduce_fusion
  301.6 0.1 select_bitcast_fusion
  301.7 0.7 copy.68
  302.4 1.3 copy.63
  (12 shorter events, 0.2 us)
Async XLA Ops:
  13.6 61.7 %collective-permute-start = (f32[2,8,32,5,256]{4,0,3,2,1:T(2,128)S(1)}, f32[2,8,32,5,256]{4,0,3,2,1:T(2,128)S(1)}, u32[]{:S(2)}, u32[]{:S(2)}) collective-permute-start(f32[2,8,32,5,256]{4,0,3,2,1:T(2,128)S(1)} %fusion.9), channel_id=1, source_target_pairs={{4,0},{8,4},{12,8},{16,12},{20,16},{24,20},{28,24},{5,1},{9,5},{13... | collective-permute-start | bytes 7864328 | tf_op jit(solution)/shard_map/ppermute | solution.py:17
  21.4 110.3 %collective-permute-start.1 = (f32[2,8,32,5,256]{4,0,3,2,1:T(2,128)S(1)}, f32[2,8,32,5,256]{4,0,3,2,1:T(2,128)S(1)}, u32[]{:S(2)}, u32[]{:S(2)}) collective-permute-start(f32[2,8,32,5,256]{4,0,3,2,1:T(2,128)S(1)} %fusion.7), channel_id=1, source_target_pairs={{0,4},{4,8},{8,12},{12,16},{16,20},{20,24},{24,28},{1,5},{5,9},{9,... | collective-permute-start | bytes 7864328 | tf_op jit(solution)/shard_map/ppermute | solution.py:17
  139.4 60.7 %collective-permute-start.2 = (bf16[2,8,32,5,256]{4,0,3,2,1:T(2,128)(2,1)S(1)}, bf16[2,8,32,5,256]{4,0,3,2,1:T(2,128)(2,1)}, u32[]{:S(2)}, u32[]{:S(2)}) collective-permute-start(bf16[2,8,32,5,256]{4,0,3,2,1:T(2,128)(2,1)S(1)} %add_convert_fusion), channel_id=1, source_target_pairs={{0,4},{4,8},{8,12},{12,16},{16,20},{20,24},{24,28},{1,5},{5,9},{9,... | collective-permute-start | bytes 3932168 | tf_op jit(solution)/shard_map/ppermute | solution.py:25
  144.9 55.2 %collective-permute-start.3 = (bf16[2,8,32,5,256]{4,0,3,2,1:T(2,128)(2,1)S(1)}, bf16[2,8,32,5,256]{4,0,3,2,1:T(2,128)(2,1)}, u32[]{:S(2)}, u32[]{:S(2)}) collective-permute-start(bf16[2,8,32,5,256]{4,0,3,2,1:T(2,128)(2,1)S(1)} %add_convert_fusion), channel_id=1, source_target_pairs={{4,0},{8,4},{12,8},{16,12},{20,16},{24,20},{28,24},{5,1},{9,5},{13... | collective-permute-start | bytes 3932168 | tf_op jit(solution)/shard_map/ppermute | solution.py:28
  224.7 8.9 %copy-start = (f32[2,256]{1,0:T(2,128)S(1)}, f32[2,256]{1,0:T(2,128)}, u32[]{:S(2)}) copy-start(f32[2,256]{1,0:T(2,128)} %param.10) | copy-start | bytes 6148
  229.9 13.7 %all-to-all-start = ((bf16[8,8,2,2,5,256]{5,1,4,3,2,0:T(8,128)(2,1)}), bf16[8,8,2,2,5,256]{5,1,4,3,2,0:T(8,128)(2,1)S(1)}, u32[]{:S(2)}, u32[]{:S(2)}) async-start(bf16[8,8,2,2,5,256]{5,1,4,3,2,0:T(8,128)(2,1)} %copy.61), calls=%async_computation | async-start | bytes 1310720 | tf_op jit(solution)/shard_map/all_to_all | solution.py:99
where the time goes:
time: 304 us
  waiting for transfers between devices  165 us (54%)
  other arithmetic  37.6 us (12%)
  blocking collectives  31.8 us (10%)
  matrix products  28 us (9%)
  local copies, waits for them, and re-layouts  22.4 us (7%)
  starting transfers between devices  17.6 us (6%)
    ppermute x2, waiting for transfers between devices, from_behind(): lax.ppermute(value, axis, [(source, source + steps) for source in range(l...  104 us
    ppermute x1, waiting for transfers between devices, padded_2(): lax.ppermute(lax.slice_in_dim(block, block.shape[dim] - width, None, axis...  50.9 us
    all_gather x1, blocking collectives, body(): lax.all_gather(local_factor.astype(jnp.bfloat16), 'slab', axis=0, tiled=T...  31.8 us
    another operation x7, other arithmetic, upper_factor(): return jnp.swapaxes(jnp.linalg.cholesky(gram), 1, 2)  23.8 us
    dot_general x3, matrix products, record_terms(): jnp.einsum('cq,cbtvp->qbtvp', select, scaled, precision=lax.Precision.HIG...  19.4 us
    all_to_all x1, waiting for transfers between devices, body(): lax.all_to_all(local_spec, 'freq', split_axis=0, concat_axis=1, tiled=True)  9.9 us
    reshape x1, local copies, waits for them, and re-layouts, body(): padded.reshape(-1, points)  8.44 us
    ppermute x2, starting transfers between devices, from_behind(): lax.ppermute(value, axis, [(source, source + steps) for source in range(l...  6.96 us
  transfers between devices with their start and end apart: 5, of which 4 were waited for; matrix products, arithmetic and copies ran while one was open for 3% of the time, Pallas kernels for 0%

commit v1 on v0

--- a/solution.py
+++ b/solution.py
@@ -96,7 +96,15 @@
     local_spec = jnp.einsum(
         "xbtvp,tkr->kbrxvp", smoothed, dft_table(), precision=lax.Precision.HIGHEST
     ).astype(jnp.bfloat16)
-    spectra = lax.all_to_all(local_spec, "freq", split_axis=0, concat_axis=1, tiled=True)
+    spectra = jnp.concatenate(
+        lax.all_to_all(
+            jnp.stack(jnp.split(local_spec, lax.axis_size("freq"), 0)),
+            axis_name="freq",
+            split_axis=0,
+            concat_axis=0,
+        ),
+        1,
+    )
     freq_count = spectra.shape[0]
     columns = 2 * spectra.shape[1]
     values = spectra.astype(jnp.float32).reshape(

time: 304 us -> 306 us (level)
  no operation moved by 1% of the time
where the time goes in v1:
time: 306 us
  waiting for transfers between devices  165 us (54%)
  other arithmetic  39.7 us (13%)
  blocking collectives  31.8 us (10%)
  matrix products  27.9 us (9%)
  local copies, waits for them, and re-layouts  22.2 us (7%)
  starting transfers between devices  17.6 us (6%)
    ppermute x2, waiting for transfers between devices, from_behind(): lax.ppermute(value, axis, [(source, source + steps) for source in range(l...  104 us
    ppermute x1, waiting for transfers between devices, padded_2(): lax.ppermute(lax.slice_in_dim(block, block.shape[dim] - width, None, axis...  50.9 us
    all_gather x1, blocking collectives, body(): lax.all_gather(local_factor.astype(jnp.bfloat16), 'slab', axis=0, tiled=T...  31.8 us
    another operation x7, other arithmetic, upper_factor(): return jnp.swapaxes(jnp.linalg.cholesky(gram), 1, 2)  23.8 us
    dot_general x3, matrix products, record_terms(): jnp.einsum('cq,cbtvp->qbtvp', select, scaled, precision=lax.Precision.HIG...  19.4 us
    all_to_all x1, waiting for transfers between devices, body(): lax.all_to_all(jnp.stack(jnp.split(local_spec, lax.axis_size('freq'), 0))...  9.9 us
    reshape x1, local copies, waits for them, and re-layouts, body(): padded.reshape(-1, points)  8.44 us
    ppermute x2, starting transfers between devices, from_behind(): lax.ppermute(value, axis, [(source, source + steps) for source in range(l...  6.96 us
  transfers between devices with their start and end apart: 5, of which 4 were waited for; matrix products, arithmetic and copies ran while one was open for 3% of the time, Pallas kernels for 0%

profile of v1, /device:TPU:0, one launch (start us, length us, event | category | flops | bytes accessed | tf_op | source)
XLA Modules:
  0.0 305.5 jit_solution(17202280778373783434)
XLA Ops:
  0.6 0.7 bitcast_convert_fusion.2
  1.3 1.4 fusion.54
  2.8 0.7 iota_compare_fusion.3
  3.5 1.0 slice_reduce_fusion.2
  4.5 3.2 %convert_multiply_fusion.2 = (f32[2,8,32,5,256]{4,2,3,1,0:T(8,128)S(1)}, f32[2,8,32,5,256]{4,2,3,1,0:T(8,128)S(1)}, f32[2,8,32,5,256]{4,2,3,1,0:T(8,128)S(1)}) fusion(f32[2,256]{1,0:T(2,128)S(1)} %get-tuple-element.21, bf16[1,3,2,8,32,5,256]{6,4,5,3,2,1,0:T(8,128)(2,1)} %param.6, f32[2,256]{1,0:T(2,128)S(1)} %get-tuple-element.22, ...), kind=kLoop, calls=%fused_computation.12 | loop fusion | flops 3932160 | bytes 11802624 | tf_op jit(solution)/shard_map/mul | solution.py:59
  7.7 5.8 %fusion.9 = f32[2,8,32,5,256]{4,0,3,2,1:T(2,128)S(1)} fusion(f32[2,8,32,5,256]{4,2,3,1,0:T(8,128)S(1)} %get-tuple-element.16, pred[2]{0:T(512)(128)(4,1)S(1)} %iota_compare_fusion.3, s32[2]{0:T(128)S(1)} %get-tuple-element.13), kind=kOutput, calls=%fused_computation.19 | convolution fusion | flops 15728648 | bytes 5242890 | tf_op jit(solution)/shard_map/cq,cbtvp->qbtvp/dot_general | solution.py:60
  13.6 1.3 collective-permute-start
  14.9 0.7 iota_compare_fusion.2
  15.5 5.8 %fusion.7 = f32[2,8,32,5,256]{4,0,3,2,1:T(2,128)S(1)} fusion(f32[2,8,32,5,256]{4,2,3,1,0:T(8,128)S(1)} %get-tuple-element.15, pred[2]{0:T(512)(128)(4,1)S(1)} %iota_compare_fusion.2, s32[2]{0:T(128)S(1)} %get-tuple-element.12), kind=kOutput, calls=%fused_computation.17 | convolution fusion | flops 15728648 | bytes 5242890 | tf_op jit(solution)/shard_map/cq,cbtvp->qbtvp/dot_general | solution.py:60
  21.4 5.7 %collective-permute-start.1 = (f32[2,8,32,5,256]{4,0,3,2,1:T(2,128)S(1)}, f32[2,8,32,5,256]{4,0,3,2,1:T(2,128)S(1)}, u32[]{:S(2)}, u32[]{:S(2)}) collective-permute-start(f32[2,8,32,5,256]{4,0,3,2,1:T(2,128)S(1)} %fusion.7), channel_id=1, source_target_pairs={{0,4},{4,8},{8,12},{12,16},{16,20},{20,24},{24,28},{1,5},{5,9},{9,... | collective-permute-start | bytes 7864328 | tf_op jit(solution)/shard_map/ppermute | solution.py:17
  27.0 0.7 iota_compare_fusion.4
  27.7 47.6 %collective-permute-done = f32[2,8,32,5,256]{4,0,3,2,1:T(2,128)S(1)} collective-permute-done((f32[2,8,32,5,256]{4,0,3,2,1:T(2,128)S(1)}, f32[2,8,32,5,256]{4,0,3,2,1:T(2,128)S(1)}, u32[]{:S(2)}, u32[]{:S(2)}) %collective-permute-start) | collective-permute-done | bytes 2621472 | tf_op jit(solution)/shard_map/ppermute | solution.py:17
  75.3 56.3 %collective-permute-done.1 = f32[2,8,32,5,256]{4,0,3,2,1:T(2,128)S(1)} collective-permute-done((f32[2,8,32,5,256]{4,0,3,2,1:T(2,128)S(1)}, f32[2,8,32,5,256]{4,0,3,2,1:T(2,128)S(1)}, u32[]{:S(2)}, u32[]{:S(2)}) %collective-permute-start.1) | collective-permute-done | bytes 2621472 | tf_op jit(solution)/shard_map/ppermute | solution.py:17
  131.6 7.8 %add_convert_fusion = bf16[2,8,32,5,256]{4,0,3,2,1:T(2,128)(2,1)S(1)} fusion(f32[2,8,32,5,256]{4,0,3,2,1:T(2,128)S(1)} %collective-permute-done.1, f32[2,8,32,5,256]{4,0,3,2,1:T(2,128)S(1)} %collective-permute-done, f32[2,8,32,5,256]{4,2,3,1,0:T(8,128)S(1)} %get-tuple-element.14, pred[2]{0:T(512)(128)(4,1)S(1)} %iota_compare_fusion.4, ...), kind=kOutput, calls=%fused_computation.16 | convolution fusion | flops 17694728 | bytes 9175050 | tf_op jit(solution)/shard_map/cq,cbtvp->qbtvp/dot_general | solution.py:60
  139.4 5.5 %collective-permute-start.2 = (bf16[2,8,32,5,256]{4,0,3,2,1:T(2,128)(2,1)S(1)}, bf16[2,8,32,5,256]{4,0,3,2,1:T(2,128)(2,1)}, u32[]{:S(2)}, u32[]{:S(2)}) collective-permute-start(bf16[2,8,32,5,256]{4,0,3,2,1:T(2,128)(2,1)S(1)} %add_convert_fusion), channel_id=1, source_target_pairs={{0,4},{4,8},{8,12},{12,16},{16,20},{20,24},{24,28},{1,5},{5,9},{9,... | collective-permute-start | bytes 3932168 | tf_op jit(solution)/shard_map/ppermute | solution.py:25
  144.9 1.5 collective-permute-start.3
  146.4 0.2 multiply_convert_fusion
  146.6 1.0 convert_element_type.143
  147.6 0.7 multiply_reduce_fusion
  149.1 0.1 cosine_multiply_fusion
  149.2 50.9 %collective-permute-done.2 = bf16[2,8,32,5,256]{4,0,3,2,1:T(2,128)(2,1)} collective-permute-done((bf16[2,8,32,5,256]{4,0,3,2,1:T(2,128)(2,1)S(1)}, bf16[2,8,32,5,256]{4,0,3,2,1:T(2,128)(2,1)}, u32[]{:S(2)}, u32[]{:S(2)}) %collective-permute-start.2) | collective-permute-done | bytes 1310752 | tf_op jit(solution)/shard_map/ppermute | solution.py:25
  200.1 0.0 collective-permute-done.3
  200.1 5.7 %pad_maximum_fusion = bf16[6,8,32,5,256]{4,0,3,2,1:T(8,128)(2,1)S(1)} fusion(bf16[2,8,32,5,256]{4,0,3,2,1:T(2,128)(2,1)} %collective-permute-done.3, bf16[2,8,32,5,256]{4,0,3,2,1:T(2,128)(2,1)S(1)} %add_convert_fusion, bf16[2,8,32,5,256]{4,0,3,2,1:T(2,128)(2,1)} %collective-permute-done.2), kind=kLoop, calls=%fused_computation | loop fusion | flops 11796480 | bytes 7864320 | tf_op jit(solution)/shard_map/concatenate | solution.py:29
  205.8 4.1 %copy.45 = bf16[6,8,32,5,256]{4,3,2,1,0:T(8,128)(2,1)} copy(bf16[6,8,32,5,256]{4,0,3,2,1:T(8,128)(2,1)S(1)} %pad_maximum_fusion) | data formatting | bytes 7864320 | tf_op jit(solution)/shard_map/concatenate | solution.py:29
  210.0 8.4 %reshape.317 = bf16[7680,256]{1,0:T(8,128)(2,1)} reshape(bf16[6,8,32,5,256]{4,3,2,1,0:T(8,128)(2,1)} %copy.45) | data formatting | bytes 7864320 | tf_op jit(solution)/shard_map/reshape | solution.py:90
  218.4 3.3 %fusion.55 = f32[7680,256]{1,0:T(8,128)S(1)} fusion(bf16[7680,256]{1,0:T(8,128)(2,1)} %reshape.317, bf16[256,256]{1,0:T(8,128)(2,1)S(1)} %convert_element_type.143), kind=kOutput, calls=%fused_computation.98 | convolution fusion | flops 1006632960 | bytes 11927552 | tf_op jit(solution)/shard_map/dot_general | solution.py:90
  221.7 0.8 fusion
  222.5 2.1 reshape.327
  224.7 4.2 %fusion.21 = bf16[8,8,2,2,5,256]{5,0,4,1,3,2:T(8,128)(2,1)S(1)} fusion(f32[2,8,32,5,256]{4,3,2,1,0:T(8,128)} %reshape.327, f32[32,8,1]{0,1,2:T(8,128)S(1)} %get-tuple-element.25, f32[32,8,1]{0,1,2:T(8,128)S(1)} %get-tuple-element.24), kind=kOutput, calls=%fused_computation.28 | convolution fusion | flops 126157312 | bytes 3278848 | tf_op jit(solution)/shard_map/xbtvp,tkr->kbrxvp/dot_general | solution.py:96
  228.9 0.0 copy-start
  228.9 0.5 slice_bitcast_fusion.3
  229.4 2.1 pad_maximum_fusion.1
  231.5 3.7 %all-to-all-start = ((bf16[4,2,8,2,2,5,256]{6,1,5,2,4,3,0:T(2,128)(2,1)}), bf16[4,2,8,2,2,5,256]{6,1,5,2,4,3,0:T(2,128)(2,1)S(1)}, u32[]{:S(2)}, u32[]{:S(2)}) async-start(bf16[4,2,8,2,2,5,256]{6,1,5,2,4,3,0:T(2,128)(2,1)} %pad_maximum_fusion.1), calls=%async_computation | async-start | bytes 1310720 | tf_op jit(solution)/shard_map/all_to_all | solution.py:100
  235.2 0.0 copy-done
  235.2 9.9 %all-to-all-done = bf16[4,2,8,2,2,5,256]{6,1,5,2,4,3,0:T(2,128)(2,1)S(1)} async-done(((bf16[4,2,8,2,2,5,256]{6,1,5,2,4,3,0:T(2,128)(2,1)}), bf16[4,2,8,2,2,5,256]{6,1,5,2,4,3,0:T(2,128)(2,1)S(1)}, u32[]{:S(2)}, u32[]{:S(2)}) %all-to-all-start) | async-done | bytes 655392 | tf_op jit(solution)/shard_map/all_to_all | solution.py:100
  245.1 0.2 copy.48
  245.4 0.1 copy.77
  245.5 0.7 reshape.320
  246.2 0.8 fusion.18
  247.0 0.1 copy.49
  247.1 11.7 %custom-call.4 = f32[2,64,64]{2,1,0:T(8,128)S(1)} custom-call(f32[2,64,64]{2,1,0:T(8,128)S(1)} %fusion.26), custom_call_target="Cholesky" | custom-call | tf_op jit(solution)/shard_map/jit(cholesky)/cholesky | solution.py:64
  258.9 0.1 compare_reduce_fusion.1
  259.0 0.1 fusion.27
  259.1 0.1 copy.50
  259.2 31.8 %all-gather = bf16[16,64,64]{2,1,0:T(8,128)(2,1)S(1)} all-gather(bf16[2,64,64]{2,1,0:T(8,128)(2,1)S(1)} %copy.50), channel_id=2, replica_groups=mesh['slab'=8,'freq'=4] {'slab'}, dimensions={0}, use_global_device_ids=true | all-gather | bytes 147456 | tf_op jit(solution)/shard_map/all_gather | solution.py:120
  291.0 0.2 convolution_bitcast_fusion
  291.2 0.1 copy.52
  291.3 11.7 %custom-call.5 = f32[2,64,64]{2,1,0:T(8,128)S(1)} custom-call(f32[2,64,64]{2,1,0:T(8,128)S(1)} %fusion.25), custom_call_target="Cholesky" | custom-call | tf_op jit(solution)/shard_map/jit(cholesky)/cholesky | solution.py:64
  303.1 0.1 compare_reduce_fusion
  303.2 0.1 select_bitcast_fusion
  303.3 0.7 copy.54
  304.0 1.5 copy.53
  (12 shorter events, 0.2 us)
Async XLA Ops:
  13.6 61.7 %collective-permute-start = (f32[2,8,32,5,256]{4,0,3,2,1:T(2,128)S(1)}, f32[2,8,32,5,256]{4,0,3,2,1:T(2,128)S(1)}, u32[]{:S(2)}, u32[]{:S(2)}) collective-permute-start(f32[2,8,32,5,256]{4,0,3,2,1:T(2,128)S(1)} %fusion.9), channel_id=1, source_target_pairs={{4,0},{8,4},{12,8},{16,12},{20,16},{24,20},{28,24},{5,1},{9,5},{13... | collective-permute-start | bytes 7864328 | tf_op jit(solution)/shard_map/ppermute | solution.py:17
  21.4 110.3 %collective-permute-start.1 = (f32[2,8,32,5,256]{4,0,3,2,1:T(2,128)S(1)}, f32[2,8,32,5,256]{4,0,3,2,1:T(2,128)S(1)}, u32[]{:S(2)}, u32[]{:S(2)}) collective-permute-start(f32[2,8,32,5,256]{4,0,3,2,1:T(2,128)S(1)} %fusion.7), channel_id=1, source_target_pairs={{0,4},{4,8},{8,12},{12,16},{16,20},{20,24},{24,28},{1,5},{5,9},{9,... | collective-permute-start | bytes 7864328 | tf_op jit(solution)/shard_map/ppermute | solution.py:17
  139.4 60.7 %collective-permute-start.2 = (bf16[2,8,32,5,256]{4,0,3,2,1:T(2,128)(2,1)S(1)}, bf16[2,8,32,5,256]{4,0,3,2,1:T(2,128)(2,1)}, u32[]{:S(2)}, u32[]{:S(2)}) collective-permute-start(bf16[2,8,32,5,256]{4,0,3,2,1:T(2,128)(2,1)S(1)} %add_convert_fusion), channel_id=1, source_target_pairs={{0,4},{4,8},{8,12},{12,16},{16,20},{20,24},{24,28},{1,5},{5,9},{9,... | collective-permute-start | bytes 3932168 | tf_op jit(solution)/shard_map/ppermute | solution.py:25
  144.9 55.2 %collective-permute-start.3 = (bf16[2,8,32,5,256]{4,0,3,2,1:T(2,128)(2,1)S(1)}, bf16[2,8,32,5,256]{4,0,3,2,1:T(2,128)(2,1)}, u32[]{:S(2)}, u32[]{:S(2)}) collective-permute-start(bf16[2,8,32,5,256]{4,0,3,2,1:T(2,128)(2,1)S(1)} %add_convert_fusion), channel_id=1, source_target_pairs={{4,0},{8,4},{12,8},{16,12},{20,16},{24,20},{28,24},{5,1},{9,5},{13... | collective-permute-start | bytes 3932168 | tf_op jit(solution)/shard_map/ppermute | solution.py:28
  228.9 6.3 %copy-start = (f32[2,256]{1,0:T(2,128)S(1)}, f32[2,256]{1,0:T(2,128)}, u32[]{:S(2)}) copy-start(f32[2,256]{1,0:T(2,128)} %param.10) | copy-start | bytes 6148
  231.5 13.7 %all-to-all-start = ((bf16[4,2,8,2,2,5,256]{6,1,5,2,4,3,0:T(2,128)(2,1)}), bf16[4,2,8,2,2,5,256]{6,1,5,2,4,3,0:T(2,128)(2,1)S(1)}, u32[]{:S(2)}, u32[]{:S(2)}) async-start(bf16[4,2,8,2,2,5,256]{6,1,5,2,4,3,0:T(2,128)(2,1)} %pad_maximum_fusion.1), calls=%async_computation | async-start | bytes 1310720 | tf_op jit(solution)/shard_map/all_to_all | solution.py:100
